TPU v7x, 32 devices: a whole 2x2x4 slice. The times are simulated.
32 devices in a mesh: blk: 2 (over x), head: 4 (over z), weight: 4 (over y, core).
Axes of the slice: x: 2, y: 2, z: 4, core: 2. Of those that a mesh axis runs over, the one named last changes fastest.
Arguments:
- hidden_in: bfloat16 [2048, 2, 768], P(('blk', 'head', 'weight')), may hold values from -6 to 6
- qkv_weight: bfloat16 [768, 2304], replicated, may hold values from -0.21875 to 0.21875
- query_bias: float32 [768], replicated, may hold values from -3 to 3
- value_bias: float32 [768], replicated, may hold values from -0.12 to 0.12
- out_weight: bfloat16 [768, 768], replicated, may hold values from -5.75 to 5.75
- out_bias: float32 [768], replicated, may hold values from -3 to 3
- norm1_gain: float32 [768], replicated, may hold values from 0.25 to 1.75
- norm1_bias: float32 [768], replicated, may hold values from -3 to 3
- up_weight: bfloat16 [768, 3072], P(None, 'weight'), may hold values from -0.21875 to 0.21875
- up_bias: float32 [3072], P('weight'), may hold values from -3 to 3
- down_weight: bfloat16 [3072, 768], P('weight'), may hold values from -0.109375 to 0.109375
- down_bias: float32 [768], replicated, may hold values from -3 to 3
- norm2_gain: float32 [768], replicated, may hold values from 0.25 to 1.75
- norm2_bias: float32 [768], replicated, may hold values from -3 to 3
- lengths: int32 [2], replicated, may hold values from 256 to 2048, as said below
- out_cotangent: bfloat16 [2048, 2, 768], P(('blk', 'head', 'weight')), may hold values from -6 to 6
Outputs:
- layer_out: bfloat16 [2048, 2, 768], P(('blk', 'head', 'weight'))
- grad_in: float32 [2048, 2, 768], P(('blk', 'head', 'weight'))
- grad_qkv_weight: float32 [768, 2304], replicated
- grad_query_bias: float32 [768], replicated
- grad_value_bias: float32 [768], replicated
- grad_out_weight: float32 [768, 768], replicated
- grad_out_bias: float32 [768], replicated
- grad_norm1_gain: float32 [768], replicated
- grad_norm1_bias: float32 [768], replicated
- grad_up_weight: float32 [768, 3072], P(None, 'weight')
- grad_up_bias: float32 [3072], P('weight')
- grad_down_weight: float32 [3072, 768], P('weight')
- grad_down_bias: float32 [768], replicated
- grad_norm2_gain: float32 [768], replicated
- grad_norm2_bias: float32 [768], replicated
Inputs may be any that keep to these rules, and one draw needn't show every extreme that they name: Positions 0 to lengths[b] - 1 of sequence b are tokens and the rest padding; at least one sequence has no padding.
All inputs are finite; a program needn't handle non-finite values.
Results may differ from a plain program's by a relative error of at most 0.02.
Values may be sent and summed in bfloat16 or wider, within the bound.
No kernel may reach another device: no remote copies, remote signals or barrier semaphores. Data moves between devices by JAX's collectives and lax.ppermute only.
A program may use at most 128 MiB of HBM per device.

v0:
```python
import jax
import jax.numpy as jnp
from jax import lax
from jax.sharding import PartitionSpec as P

HEADS = 12
HEAD_DIM = 64
EPS = 1e-05
SQRT_HALF = 0.7071067811865476
INV_ROOT_TAU = 0.3989422804014327


def norm_forward(resid, gain, bias):
    centre = jnp.mean(resid, axis=-1, keepdims=True)
    centred = resid - centre
    spread = jnp.mean(centred * centred, axis=-1, keepdims=True)
    rstd = lax.rsqrt(spread + EPS)
    normed = centred * rstd
    return (normed * gain + bias, normed, rstd)


def norm_backward(grad, normed, rstd, gain):
    scaled = grad * gain
    inner = (
        scaled
        - jnp.mean(scaled, axis=-1, keepdims=True)
        - normed * jnp.mean(scaled * normed, axis=-1, keepdims=True)
    )
    return (rstd * inner, jnp.sum(grad * normed, axis=0), jnp.sum(grad, axis=0))


def gelu_value(pre):
    return 0.5 * pre * (1.0 + jax.scipy.special.erf(pre * SQRT_HALF))


def gelu_slope(pre):
    return (
        0.5 * (1.0 + jax.scipy.special.erf(pre * SQRT_HALF))
        + pre * jnp.exp(-0.5 * pre * pre) * INV_ROOT_TAU
    )


def sweep(step, carry, piece):
    count = jax.tree.leaves(piece)[0].shape[0]
    size = 1024

    def advance(index, state):
        part = jax.tree.map(
            lambda leaf: lax.dynamic_slice_in_dim(leaf, index * size, size, 0), piece
        )
        return step(state, part, index * size)

    return lax.fori_loop(0, count // size, advance, carry)


def per_device(
    hidden_in,
    qkv_weight,
    query_bias,
    value_bias,
    out_weight,
    out_bias,
    norm1_gain,
    norm1_bias,
    up_weight,
    up_bias,
    down_weight,
    down_bias,
    norm2_gain,
    norm2_bias,
    lengths,
    out_cotangent,
):
    rows_here, seq_count, width = hidden_in.shape
    head_devs = lax.axis_size("head")
    weight_devs = lax.axis_size("weight")
    group = width // head_devs
    local_heads = HEADS // head_devs
    scale = HEAD_DIM ** (-0.5)
    tokens = rows_here * seq_count
    flat = hidden_in.reshape(tokens, width)
    bias_all = jnp.concatenate([query_bias, jnp.zeros((width,), jnp.float32), value_bias])
    packed = (jnp.dot(flat, qkv_weight, preferred_element_type=jnp.float32) + bias_all).astype(
        jnp.bfloat16
    )
    packed = packed.reshape(rows_here, seq_count, 3, width)
    regrouped = lax.all_to_all(packed, "head", split_axis=3, concat_axis=0, tiled=True)
    query_rows = regrouped.shape[0]
    query = regrouped[:, :, 0].reshape(query_rows, seq_count, local_heads, HEAD_DIM)
    keyval = regrouped[:, :, 1:]
    key_total = query_rows * lax.axis_size("blk") * weight_devs

    def positions(start, count):
        index = jnp.arange(count, dtype=jnp.int32) + start
        device = index // query_rows
        within = index % query_rows
        source = device // weight_devs * head_devs + within // rows_here
        return (source * weight_devs + device % weight_devs) * rows_here + within % rows_here

    def split_block(block, start):
        count = block.shape[0]
        keys = block[:, :, 0].reshape(count, seq_count, local_heads, HEAD_DIM)
        values = block[:, :, 1].reshape(count, seq_count, local_heads, HEAD_DIM)
        valid = positions(start, count)[None, :] < lengths[:, None]
        scores = (
            jnp.einsum("qbhe,kbhe->bhqk", query, keys, preferred_element_type=jnp.float32) * scale
        )
        weights = jnp.where(valid[:, None, None, :], jnp.exp(scores), 0.0)
        return (keys, values, weights)

    def forward_block(carry, block, start):
        numer, denom = carry
        keys, values, weights = split_block(block, start)
        numer = numer + jnp.einsum(
            "bhqk,kbhe->qbhe",
            weights.astype(jnp.bfloat16),
            values,
            preferred_element_type=jnp.float32,
        )
        return (numer, denom + jnp.sum(weights, axis=-1))

    first = (
        jnp.zeros((query_rows, seq_count, local_heads, HEAD_DIM), jnp.float32),
        jnp.zeros((seq_count, local_heads, query_rows), jnp.float32),
    )
    numer, denom = sweep(
        forward_block, first, lax.all_gather(keyval, ("blk", "weight"), axis=0, tiled=True)
    )
    attended = (numer / jnp.transpose(denom, (2, 0, 1))[..., None]).astype(jnp.bfloat16)
    returned = lax.all_to_all(
        attended.reshape(query_rows, seq_count, group),
        "head",
        split_axis=0,
        concat_axis=2,
        tiled=True,
    )
    attn_flat = returned.reshape(tokens, width)
    resid1 = (
        flat.astype(jnp.float32)
        + jnp.dot(attn_flat, out_weight, preferred_element_type=jnp.float32)
        + out_bias
    )
    hidden1, normed1, rstd1 = norm_forward(resid1, norm1_gain, norm1_bias)
    hidden_half = hidden1.astype(jnp.bfloat16).reshape(rows_here, seq_count, width)
    gathered = lax.all_gather(hidden_half, "weight", axis=0, tiled=True)
    gathered_flat = gathered.reshape(weight_devs * tokens, width)
    pre = jnp.dot(gathered_flat, up_weight, preferred_element_type=jnp.float32) + up_bias
    active = gelu_value(pre).astype(jnp.bfloat16)
    active_rows = active.reshape(weight_devs * rows_here, seq_count, -1)
    count = lax.axis_size("weight") * rows_here
    part = active_rows
    mixed = (
        lax.psum_scatter(
            jnp.dot(
                part.reshape(count * seq_count, -1), down_weight, preferred_element_type=jnp.float32
            )
            .reshape(count, seq_count, width)
            .astype(jnp.bfloat16),
            "weight",
            scatter_dimension=0,
            tiled=True,
        )
        .astype(jnp.float32)
        .reshape(tokens, width)
    )
    resid2 = hidden1 + mixed + down_bias
    final, normed2, rstd2 = norm_forward(resid2, norm2_gain, norm2_bias)
    layer_out = final.astype(jnp.bfloat16).reshape(rows_here, seq_count, width)
    cotangent = out_cotangent.reshape(tokens, width).astype(jnp.float32)
    grad_resid2, grad_norm2_gain, grad_norm2_bias = norm_backward(
        cotangent, normed2, rstd2, norm2_gain
    )
    grad_down_bias = jnp.sum(grad_resid2, axis=0)
    grad_mixed = grad_resid2.astype(jnp.bfloat16).reshape(rows_here, seq_count, width)
    mixed_all = lax.all_gather(grad_mixed, "weight", axis=0, tiled=True).reshape(
        weight_devs * tokens, width
    )
    grad_down_weight = jnp.dot(active.T, mixed_all, preferred_element_type=jnp.float32)
    grad_pre = jnp.dot(mixed_all, down_weight.T, preferred_element_type=jnp.float32) * gelu_slope(
        pre
    )
    grad_up_bias = jnp.sum(grad_pre, axis=0)
    grad_pre_half = grad_pre.astype(jnp.bfloat16)
    grad_up_weight = jnp.dot(gathered_flat.T, grad_pre_half, preferred_element_type=jnp.float32)
    pre_rows = grad_pre_half.reshape(weight_devs * rows_here, seq_count, -1)
    count = lax.axis_size("weight") * rows_here
    part = pre_rows
    back_hidden = (
        lax.psum_scatter(
            jnp.dot(
                part.reshape(count * seq_count, -1), up_weight.T, preferred_element_type=jnp.float32
            )
            .reshape(count, seq_count, width)
            .astype(jnp.bfloat16),
            "weight",
            scatter_dimension=0,
            tiled=True,
        )
        .astype(jnp.float32)
        .reshape(tokens, width)
    )
    grad_hidden1 = grad_resid2 + back_hidden
    grad_resid1, grad_norm1_gain, grad_norm1_bias = norm_backward(
        grad_hidden1, normed1, rstd1, norm1_gain
    )
    grad_out_bias = jnp.sum(grad_resid1, axis=0)
    grad_attn_half = grad_resid1.astype(jnp.bfloat16)
    grad_out_weight = jnp.dot(attn_flat.T, grad_attn_half, preferred_element_type=jnp.float32)
    grad_attended = jnp.dot(
        grad_attn_half, out_weight.T, preferred_element_type=jnp.float32
    ).astype(jnp.bfloat16)
    heads_grad = lax.all_to_all(
        grad_attended.reshape(rows_here, seq_count, width),
        "head",
        split_axis=2,
        concat_axis=0,
        tiled=True,
    )
    heads_grad = heads_grad.reshape(query_rows, seq_count, local_heads, HEAD_DIM)
    delta = jnp.transpose(
        jnp.sum(heads_grad.astype(jnp.float32) * attended.astype(jnp.float32), axis=-1), (1, 2, 0)
    )
    own_start = lax.axis_index(("blk", "weight")) * query_rows
    own_keys = keyval[:, :, 0].reshape(query_rows, seq_count, local_heads, HEAD_DIM)
    own_values = keyval[:, :, 1].reshape(query_rows, seq_count, local_heads, HEAD_DIM)
    own_valid = positions(own_start, query_rows)[None, :] < lengths[:, None]
    delta_rows = jnp.transpose(delta, (2, 0, 1))
    denom_rows = jnp.transpose(denom, (2, 0, 1))

    def key_side(carry, pieces, start):
        key_acc, value_acc, query_sums = carry
        query_piece, grad_piece, delta_piece, denom_piece = pieces
        count = query_piece.shape[0]
        scores = (
            jnp.einsum("qbhe,kbhe->bhqk", query_piece, own_keys, preferred_element_type=jnp.float32)
            * scale
        )
        weights = jnp.where(own_valid[:, None, None, :], jnp.exp(scores), 0.0)
        probs = weights / jnp.transpose(denom_piece, (1, 2, 0))[..., None]
        grad_prob = jnp.einsum(
            "qbhe,kbhe->bhqk", grad_piece, own_values, preferred_element_type=jnp.float32
        )
        score_half = (
            probs * (grad_prob - jnp.transpose(delta_piece, (1, 2, 0))[..., None])
        ).astype(jnp.bfloat16)
        value_acc = value_acc + jnp.einsum(
            "bhqk,qbhe->kbhe",
            probs.astype(jnp.bfloat16),
            grad_piece,
            preferred_element_type=jnp.float32,
        )
        key_acc = (
            key_acc
            + jnp.einsum(
                "bhqk,qbhe->kbhe", score_half, query_piece, preferred_element_type=jnp.float32
            )
            * scale
        )
        query_part = (
            jnp.einsum("bhqk,kbhe->qbhe", score_half, own_keys, preferred_element_type=jnp.float32)
            * scale
        )
        query_sums = lax.dynamic_update_slice_in_dim(
            query_sums, query_part.reshape(count, seq_count, group), start, 0
        )
        return (key_acc, value_acc, query_sums)

    second = (
        jnp.zeros((query_rows, seq_count, local_heads, HEAD_DIM), jnp.float32),
        jnp.zeros((query_rows, seq_count, local_heads, HEAD_DIM), jnp.float32),
        jnp.zeros((key_total, seq_count, group), jnp.float32),
    )
    key_acc, value_acc, query_sums = sweep(
        key_side,
        second,
        (
            lax.all_gather(query, ("blk", "weight"), axis=0, tiled=True),
            lax.all_gather(heads_grad, ("blk", "weight"), axis=0, tiled=True),
            lax.all_gather(
                delta_rows.astype(jnp.bfloat16), ("blk", "weight"), axis=0, tiled=True
            ).astype(jnp.float32),
            lax.all_gather(
                denom_rows.astype(jnp.bfloat16), ("blk", "weight"), axis=0, tiled=True
            ).astype(jnp.float32),
        ),
    )
    query_grad = lax.psum_scatter(
        query_sums.astype(jnp.bfloat16), ("blk", "weight"), scatter_dimension=0, tiled=True
    ).astype(jnp.float32)
    key_grad = key_acc.reshape(query_rows, seq_count, group)
    value_grad = value_acc.reshape(query_rows, seq_count, group)
    stacked = jnp.stack([query_grad, key_grad, value_grad], axis=2).astype(jnp.bfloat16)
    grad_packed = lax.all_to_all(stacked, "head", split_axis=0, concat_axis=3, tiled=True).reshape(
        tokens, 3 * width
    )
    grad_qkv_weight = jnp.dot(flat.T, grad_packed, preferred_element_type=jnp.float32)
    column_sums = jnp.sum(grad_packed.astype(jnp.float32), axis=0)
    grad_in = (
        jnp.dot(grad_packed, qkv_weight.T, preferred_element_type=jnp.float32) + grad_resid1
    ).reshape(rows_here, seq_count, width)
    shared = lax.psum(
        (
            grad_qkv_weight,
            column_sums[:width],
            column_sums[2 * width :],
            grad_out_weight,
            grad_out_bias,
            grad_norm1_gain,
            grad_norm1_bias,
            grad_norm2_gain,
            grad_norm2_bias,
            grad_down_bias,
        ),
        ("blk", "head", "weight"),
    )
    hidden_sums = (
        lax.psum(grad_up_weight.astype(jnp.bfloat16), ("blk", "head")).astype(jnp.float32),
        lax.psum(grad_up_bias.astype(jnp.bfloat16), ("blk", "head")).astype(jnp.float32),
        lax.psum(grad_down_weight.astype(jnp.bfloat16), ("blk", "head")).astype(jnp.float32),
    )
    return (
        layer_out,
        grad_in,
        shared[0],
        shared[1],
        shared[2],
        shared[3],
        shared[4],
        shared[5],
        shared[6],
        hidden_sums[0],
        hidden_sums[1],
        hidden_sums[2],
        shared[9],
        shared[7],
        shared[8],
    )


def solution(mesh):
    placed = (
        P(("blk", "head", "weight"), None, None),
        P(),
        P(),
        P(),
        P(),
        P(),
        P(),
        P(),
        P(None, "weight"),
        P("weight"),
        P("weight", None),
        P(),
        P(),
        P(),
        P(),
        P(("blk", "head", "weight"), None, None),
    )
    return jax.shard_map(
        per_device,
        mesh=mesh,
        in_specs=placed,
        out_specs=(
            P(("blk", "head", "weight"), None, None),
            P(("blk", "head", "weight"), None, None),
            P(),
            P(),
            P(),
            P(),
            P(),
            P(),
            P(),
            P(None, "weight"),
            P("weight"),
            P("weight", None),
            P(),
            P(),
            P(),
        ),
        check_vma=False,
    )
```

profile of v0, /device:TPU:0, one launch (start us, length us, event | category | flops | bytes accessed | tf_op | source)
XLA Modules:
  0.0 749.1 jit_solution(972970801593629136)
XLA Ops:
  9.8 2.4 fusion.47
  14.1 4.8 copy.83
  18.9 2.7 reshape.378
  21.6 22.3 %all_to_all.63 = bf16[4,2,36864]{2,1,0:T(2,128)(2,1)} all-to-all(bf16[4,2,36864]{2,1,0:T(2,128)(2,1)} %reshape.378), channel_id=1, replica_groups=mesh['blk'=2,'head'=4,'weight'=4] {'head'}, dimensions={0} | all-to-all | bytes 1179648 | tf_op jit(solution)/shard_map/all_to_all | solution.py:87
  43.9 2.6 reshape.379
  46.6 4.8 copy.101
  54.5 2.0 fusion.66
  58.3 32.0 %all-gather.4.cloned.1.call-done = bf16[2048,2,2,192]{3,0,2,1:T(8,128)(2,1)} async-done(((bf16[256,2,2,192]{3,0,2,1:T(8,128)(2,1)}), bf16[2048,2,2,192]{3,0,2,1:T(8,128)(2,1)}) %all-gather.4.cloned.1.call-update) | async-done | bytes 3145744 | tf_op jit(solution)/shard_map/all_gather | solution.py:127
  90.3 6.1 copy.87
  96.4 23.1 %while.37 = (s32[]{:T(128)}, f32[256,2,3,64]{0,3,2,1:T(8,128)}, f32[2,3,256]{2,1,0:T(4,128)S(1)}, bf16[2048,2,2,192]{0,3,1,2:T(8,128)(2,1)}, s32[2]{0:T(128)}, /...) while((s32[]{:T(128)}, f32[256,2,3,64]{0,3,2,1:T(8,128)}, ...), condition=%wide.region_2.3_spmd.clone, body=%wide.region_0.2_spmd.clone.sunk | while | flops 412356096 | bytes 19118340 | solution.py:53
  96.4 2.4 constant_dynamic-slice_fusion.3
  99.6 3.5 bitcast_reduce_fusion.2
  103.1 4.8 fusion.121
  107.9 2.4 constant_dynamic-slice_fusion.3
  111.1 3.5 bitcast_reduce_fusion.2
  114.6 4.9 fusion.121
  123.0 13.9 %all_to_all.64 = bf16[256,2,192]{2,1,0:T(2,128)(2,1)S(1)} all-to-all(bf16[256,2,192]{2,1,0:T(2,128)(2,1)} %copy.88), channel_id=1, replica_groups=mesh['blk'=2,'head'=4,'weight'=4] {'head'}, dimensions={0} | all-to-all | bytes 393216 | tf_op jit(solution)/shard_map/all_to_all | solution.py:130
  145.3 9.5 %all_gather.22 = bf16[256,2,768]{2,1,0:T(2,128)(2,1)} all-gather(bf16[64,2,768]{2,1,0:T(2,128)(2,1)} %reshape.355), channel_id=1, replica_groups=mesh['blk'=2,'head'=4,'weight'=4] {'weight'}, dimensions={0}, use_global_device_ids=true | all-gather | bytes 983040 | tf_op jit(solution)/shard_map/all_gather | solution.py:145
  154.8 3.0 reshape.356
  157.7 3.6 multiply_convert_fusion.1
  163.9 2.9 convert_element_type.130
  174.6 26.6 %all-reduce.10.cloned.1.call-done = bf16[256,2,768]{2,1,0:T(2,128)(2,1)} async-done(((bf16[256,2,768]{2,1,0:T(2,128)(2,1)}), bf16[256,2,768]{2,1,0:T(2,128)(2,1)}) %all-reduce.10.cloned.1.call-update) | async-done | bytes 786448
  203.0 2.0 reshape.369
  212.0 9.3 %all_gather.25 = bf16[256,2,768]{2,1,0:T(2,128)(2,1)} all-gather(bf16[64,2,768]{2,1,0:T(2,128)(2,1)} %reshape.360), channel_id=1, replica_groups=mesh['blk'=2,'head'=4,'weight'=4] {'weight'}, dimensions={0}, use_global_device_ids=true | all-gather | bytes 983040 | tf_op jit(solution)/shard_map/all_gather | solution.py:175
  221.3 3.0 reshape.361
  224.3 3.8 fusion.69
  230.7 2.8 convert_element_type.140
  234.2 35.0 %all-reduce.12.cloned.1.call-done = bf16[256,2,768]{2,1,0:T(2,128)(2,1)} async-done(((bf16[256,2,768]{2,1,0:T(2,128)(2,1)}), bf16[256,2,768]{2,1,0:T(2,128)(2,1)}) %all-reduce.12.cloned.1.call-update) | async-done | bytes 786448
  271.0 2.0 reshape.372
  273.0 2.2 multiply_reduce_fusion.1
  280.3 2.0 copy.92
  282.3 2.0 reshape.380
  284.3 11.5 %all_to_all.65 = bf16[4,2,12288]{2,1,0:T(2,128)(2,1)} all-to-all(bf16[4,2,12288]{2,1,0:T(2,128)(2,1)} %reshape.380), channel_id=1, replica_groups=mesh['blk'=2,'head'=4,'weight'=4] {'head'}, dimensions={0} | all-to-all | bytes 393216 | tf_op jit(solution)/shard_map/all_to_all | solution.py:212
  297.8 2.0 copy.105
  299.8 2.0 reshape.365
  305.5 8.9 %all_gather.24 = bf16[2048,2,3]{0,2,1:T(4,128)(2,1)S(1)} all-gather(bf16[256,2,3]{0,2,1:T(4,128)(2,1)S(1)} %bitcast_convert_fusion.6), channel_id=1, replica_groups=mesh['blk'=2,'head'=4,'weight'=4] {'blk','weight'}, dimensions={0}, use_global_device_ids=true | all-gather | bytes 27648 | tf_op jit(solution)/shard_map/all_gather | solution.py:282
  316.2 8.6 %all_gather.27 = bf16[2048,2,3]{0,2,1:T(4,128)(2,1)S(1)} all-gather(bf16[256,2,3]{0,2,1:T(4,128)(2,1)S(1)} %multiply_reduce_fusion.2), channel_id=1, replica_groups=mesh['blk'=2,'head'=4,'weight'=4] {'blk','weight'}, dimensions={0}, use_global_device_ids=true | all-gather | bytes 27648 | tf_op jit(solution)/shard_map/all_gather | solution.py:279
  327.4 38.4 %while.38 = (s32[]{:T(128)}, f32[256,2,3,64]{0,3,2,1:T(8,128)}, f32[256,2,3,64]{0,3,2,1:T(8,128)}, bf16[2048,2,192]{0,2,1:T(8,128)(2,1)}, bf16[2048,2,3,64]{0,3,...) while((s32[]{:T(128)}, f32[256,2,3,64]{0,3,2,1:T(8,128)}, ...), condition=%wide.region_15.16_spmd.clone, body=%wide.region_14.15_spmd.clone.sunk | while | flops 1018921472 | bytes 103770656 | solution.py:53
  329.0 3.7 select_divide_fusion.2
  332.7 3.3 multiply_convert_fusion.3
  336.4 3.7 fusion.132
  340.1 3.7 fusion.133
  348.1 3.7 select_divide_fusion.2
  351.9 3.3 multiply_convert_fusion.3
  355.5 3.8 fusion.132
  359.3 3.7 fusion.133
  365.9 3.3 convolution_convert_fusion.1
  374.6 29.7 %reduce-scatter.2.cloned.1.call-done = bf16[256,2,192]{0,2,1:T(8,128)(2,1)} async-done(((bf16[2048,2,192]{0,2,1:T(8,128)(2,1)}), bf16[256,2,192]{0,2,1:T(8,128)(2,1)}) %reduce-scatter.2.cloned.1.call-update) | async-done | bytes 196624 | tf_op jit(solution)/shard_map/reduce_scatter | solution.py:287
  404.3 2.0 pad_maximum_fusion
  406.3 3.0 copy.96
  409.3 4.6 all-to-all-start.3
  413.9 3.0 fusion.57
  416.9 37.5 %all-to-all-done.3 = bf16[256,2,3,192]{3,1,2,0:T(2,128)(2,1)} async-done(((bf16[256,2,3,192]{3,1,2,0:T(2,128)(2,1)}), bf16[256,2,3,192]{3,1,2,0:T(2,128)(2,1)}, u32[]{:S(2)}, u32[]{:S(2)}) %all-to-all-start.3) | async-done | bytes 589856 | tf_op jit(solution)/shard_map/all_to_all | solution.py:293
  458.1 2.6 reshape.366
  460.7 5.2 convolution_bitcast_fusion
  467.6 19.1 %psum.99 = bf16[768]{0:T(1024)(128)(2,1)S(1)} all-reduce(bf16[768]{0:T(1024)(128)(2,1)S(1)} %copy-done.35), channel_id=1, replica_groups=mesh['blk'=2,'head'=4,'weight'=4] {'blk','head'}, use_global_device_ids=true, to_apply=%region_30.31 | all-reduce | flops 768 | bytes 3072 | tf_op jit(solution)/shard_map/psum | solution.py:318
  487.3 45.9 %all-reduce.16.cloned.1.call-done = (bf16[768,768]{1,0:T(8,128)(2,1)}, bf16[768,768]{1,0:T(8,128)(2,1)}) async-done(((bf16[768,768]{1,0:T(8,128)(2,1)}, bf16[768,768]{1,0:T(8,128)(2,1)}), (bf16[768,768]{1,0:T(8,128)(2,1)}, bf16[768,768]{1,0:T(8,128)(2,1)})) %all-reduce.16.cloned.1.call-update) | async-done | bytes 2359312 | tf_op jit(solution)/shard_map/psum | solution.py:317
  533.3 2.9 convert_element_type.150
  537.8 2.0 convolution_add_fusion.3
  539.8 2.0 reshape.367
  546.5 42.4 %all-reduce.2 = (f32[768]{0:T(1024)}, f32[768]{0:T(1024)}, f32[768]{0:T(1024)}, f32[768]{0:T(1024)}, f32[768]{0:T(1024)}, /*index=5*/f32[768]{0:T(1024)}, f32[768]{0:T(1024)}, f32[768]{0:T(1024)}) all-reduce(f32[768]{0:T(1024)} %slice.53, f32[768]{0:T(1024)} %slice.55, ...), channel_id=1, replica_groups=mesh['blk'=2,'head'=4,'weight'=4] {'blk','head','weight'}, use_global_device_ids=true, to_apply=%region_19.20 | all-reduce | flops 6144 | bytes 49152 | tf_op jit(solution)/shard_map/psum | solution.py:301
  588.9 142.2 %all-reduce.14.cloned.1.call-done = (f32[768,2304]{0,1:T(8,128)}, f32[768,768]{1,0:T(8,128)}) async-done(((f32[768,2304]{0,1:T(8,128)}, f32[768,768]{1,0:T(8,128)}), (f32[768,2304]{0,1:T(8,128)}, f32[768,768]{1,0:T(8,128)})) %all-reduce.14.cloned.1.call-update) | async-done | bytes 9437200 | tf_op jit(solution)/shard_map/psum | solution.py:301
  731.1 8.0 %copy.99 = f32[768,2304]{1,0:T(8,128)} copy(f32[768,2304]{0,1:T(8,128)} %get-tuple-element.630) | data formatting | bytes 14155776
  739.1 3.2 copy.134
  (205 shorter events, 88.1 us)
Async XLA Ops:
  7.2 2.6 copy-start
  7.2 83.1 %all-gather.4.cloned.1.call-start = ((), (), s32[]{:S(2)}) async-start(), calls=%async_computation.5 | async-start | bytes 4718592 | tf_op jit(solution)/shard_map/all_gather | solution.py:127
  52.7 0.9 copy-start.17
  54.4 146.7 %all-reduce.10.cloned.1.call-start = ((), (), s32[]{:S(2)}) async-start(), calls=%async_computation.9 | async-start | bytes 1572864
  96.4 3.2 copy-start.22
  99.6 3.5 copy-start.24
  107.9 3.2 copy-start.22
  111.1 3.5 copy-start.24
  136.9 5.9 copy-start.25
  136.9 5.9 copy-start.27
  141.5 0.8 copy-start.7
  141.5 0.7 copy-start.31
  142.3 0.5 copy-start.32
  143.6 14.1 %copy-start.38 = (f32[768]{0:T(1024)S(1)}, f32[768]{0:T(1024)}, u32[]{:S(2)}) copy-start(f32[768]{0:T(1024)} %param.29) | copy-start | bytes 9220
  157.7 4.5 copy-start.36
  161.4 0.9 copy-start.39
  163.9 4.9 copy-start.26
  166.8 102.4 %all-reduce.12.cloned.1.call-start = ((), (), s32[]{:S(2)}) async-start(), calls=%async_computation.10 | async-start | bytes 1572864
  205.0 1.7 copy-start.20
  205.0 2.4 copy-start.33
  205.0 2.4 copy-start.34
  208.9 0.7 copy-start.19
  224.3 4.7 copy-start.37
  228.0 1.0 copy-start.41
  233.6 91.8 %all-gather.6.cloned.1.call-start = ((), (), s32[]{:S(2)}) async-start(), calls=%async_computation.6 | async-start | bytes 1769472 | tf_op jit(solution)/shard_map/all_gather | solution.py:277
  234.1 92.0 %all-gather.8.cloned.1.call-start = ((), (), s32[]{:S(2)}) async-start(), calls=%async_computation.7 | async-start | bytes 1769472 | tf_op jit(solution)/shard_map/all_gather | solution.py:278
  273.0 2.2 copy-start.8
  273.0 4.4 copy-start.18
  276.7 0.7 copy-start.15
  301.9 102.4 %reduce-scatter.2.cloned.1.call-start = ((), (), s32[]{:S(2)}) async-start(), calls=%async_computation.8 | async-start | bytes 1769472 | tf_op jit(solution)/shard_map/reduce_scatter | solution.py:287
  328.9 3.8 copy-start.3
  328.9 3.8 copy-start.12
  332.7 3.7 copy-start.2
  336.3 3.7 copy-start.4
  336.4 3.7 copy-start.5
  340.1 3.8 copy-start.1
  340.1 3.8 copy-start.10
  343.8 1.1 copy-start.6
  343.8 1.5 copy-start.13
  345.5 1.1 copy-start.14
  348.1 3.8 copy-start.3
  348.1 3.8 copy-start.12
  351.9 3.7 copy-start.2
  355.5 3.8 copy-start.4
  355.5 3.8 copy-start.5
  359.3 3.8 copy-start.1
  359.3 3.8 copy-start.10
  363.0 1.1 copy-start.6
  363.1 1.5 copy-start.13
  364.7 1.1 copy-start.14
  365.9 167.4 %all-reduce.16.cloned.1.call-start = ((), (), s32[]{:S(2)}) async-start(), calls=%async_computation.12 | async-start | bytes 4718592 | tf_op jit(solution)/shard_map/psum | solution.py:317
  365.9 3.3 copy-start.23
  365.9 3.3 copy-start.40
  409.3 45.2 %all-to-all-start.3 = ((bf16[256,2,3,192]{3,1,2,0:T(2,128)(2,1)}), bf16[256,2,3,192]{3,1,2,0:T(2,128)(2,1)}, u32[]{:S(2)}, u32[]{:S(2)}) async-start(bf16[256,2,3,192]{3,1,2,0:T(2,128)(2,1)} %copy.96), calls=%async_computation.4 | async-start | bytes 1572864 | tf_op jit(solution)/shard_map/all_to_all | solution.py:293
  413.9 317.2 %all-reduce.14.cloned.1.call-start = ((), (), s32[]{:S(2)}) async-start(), calls=%async_computation.11 | async-start | bytes 18874368 | tf_op jit(solution)/shard_map/psum | solution.py:301
  455.7 0.9 copy-start.11
  465.9 1.7 copy-start.35
  533.3 2.9 copy-start.21
  536.2 1.6 copy-start.9
  536.2 1.6 copy-start.16
  539.8 6.6 copy-start.28
  539.8 6.6 copy-start.29
  539.8 6.6 copy-start.30
Sparse Core Ops, SparseCore 0:
  54.6 35.6 all-gather.3
  166.9 34.1 all-reduce.9
  233.7 35.4 all-reduce.11
  270.9 25.7 all-gather.5
  302.0 24.0 all-gather.7
  366.0 38.2 reduce-scatter.1
  408.4 124.7 all-reduce.15
  539.8 191.2 all-reduce.13
where the time goes:
time: 752 us; the launch traced here: 749 us
  waiting for transfers between devices  350 us (47%)
  blocking collectives  146 us (19%)
  local copies, waits for them, and re-layouts  118 us (16%)
  matrix products  79.5 us (11%)
  other arithmetic  35 us (5%)
  between operations  15.1 us (2%)
    psum x1, waiting for transfers between devices, per_device(): lax.psum((grad_qkv_weight, column_sums[:width], column_sums[2 * width:],...  142 us
    unnamed x10, waiting for transfers between devices  62.2 us
    psum x1, waiting for transfers between devices, per_device(): lax.psum(grad_up_weight.astype(jnp.bfloat16), ('blk', 'head'))  45.9 us
    psum x1, blocking collectives, per_device(): lax.psum((grad_qkv_weight, column_sums[:width], column_sums[2 * width:],...  42.4 us
    all_to_all x1, waiting for transfers between devices, per_device(): lax.all_to_all(stacked, 'head', split_axis=0, concat_axis=3, tiled=True)  37.5 us
    unnamed x68, local copies, waits for them, and re-layouts  34.1 us
    all_gather x1, waiting for transfers between devices, per_device(): lax.all_gather(keyval, ('blk', 'weight'), axis=0, tiled=True)  32 us
    reduce_scatter x1, waiting for transfers between devices, per_device(): lax.psum_scatter(query_sums.astype(jnp.bfloat16), ('blk', 'weight'), scat...  29.7 us
  transfers between devices with their start and end apart: 9, of which 8 were waited for; matrix products, arithmetic and copies ran while one was open for 11% of the time, Pallas kernels for 0%

commit v1 on v0

--- a/solution.py
+++ b/solution.py
@@ -8,6 +8,11 @@
 EPS = 1e-05
 SQRT_HALF = 0.7071067811865476
 INV_ROOT_TAU = 0.3989422804014327
+
+
+def summed_here(x, name):
+    pieces = lax.all_gather(x, name)
+    return jnp.sum(pieces, axis=0)
 
 
 def norm_forward(resid, gain, bias):
@@ -314,7 +319,7 @@
         ("blk", "head", "weight"),
     )
     hidden_sums = (
-        lax.psum(grad_up_weight.astype(jnp.bfloat16), ("blk", "head")).astype(jnp.float32),
+        summed_here(grad_up_weight.astype(jnp.bfloat16), ("blk", "head")).astype(jnp.float32),
         lax.psum(grad_up_bias.astype(jnp.bfloat16), ("blk", "head")).astype(jnp.float32),
         lax.psum(grad_down_weight.astype(jnp.bfloat16), ("blk", "head")).astype(jnp.float32),
     )

time: 752 us -> 865 us (1.15)
  waiting for transfers between devices: 350 us -> 455 us
    all_gather x0 -> x1, waiting for transfers between devices: none -> 132 us  [summed_here(): pieces = lax.all_gather(x, name)]
    psum x1, waiting for transfers between devices: 45.9 us -> 24.9 us  [per_device(): lax.psum(grad_down_weight.astype(jnp.bfloat16), ('blk', 'head'))]
    all_to_all x1, waiting for transfers between devices: 37.5 us -> 24.4 us  [per_device(): lax.all_to_all(stacked, 'head', split_axis=0, concat_axis=3, tiled=True)]
    unnamed x68 -> x64, local copies, waits for them, and re-layouts: 34.1 us -> 32.2 us
    unnamed x10 -> x11, waiting for transfers between devices: 62.2 us -> 62.2 us
  transfers between devices with their start and end apart: 9 -> 10, of which waited for: 8 -> 9; matrix products, arithmetic and copies ran while one was open for 11% -> 10% of each run, Pallas kernels for 0% -> 0%
where the time goes in v1:
time: 865 us; the launch traced here: 862 us
  waiting for transfers between devices  455 us (53%)
  blocking collectives  146 us (17%)
  local copies, waits for them, and re-layouts  117 us (14%)
  matrix products  80.5 us (9%)
  other arithmetic  42.7 us (5%)
  between operations  14.8 us (2%)
    psum x1, waiting for transfers between devices, per_device(): lax.psum((grad_qkv_weight, column_sums[:width], column_sums[2 * width:],...  144 us
    all_gather x1, waiting for transfers between devices, summed_here(): pieces = lax.all_gather(x, name)  132 us
    unnamed x11, waiting for transfers between devices  62.2 us
    psum x1, blocking collectives, per_device(): lax.psum((grad_qkv_weight, column_sums[:width], column_sums[2 * width:],...  42.9 us
    reduce_scatter x1, waiting for transfers between devices, per_device(): lax.psum_scatter(query_sums.astype(jnp.bfloat16), ('blk', 'weight'), scat...  35 us
    unnamed x64, local copies, waits for them, and re-layouts  32.2 us
    all_gather x1, waiting for transfers between devices, per_device(): lax.all_gather(keyval, ('blk', 'weight'), axis=0, tiled=True)  32 us
    psum x1, waiting for transfers between devices, per_device(): lax.psum(grad_down_weight.astype(jnp.bfloat16), ('blk', 'head'))  24.9 us
  transfers between devices with their start and end apart: 10, of which 9 were waited for; matrix products, arithmetic and copies ran while one was open for 10% of the time, Pallas kernels for 0%

profile of v1, /device:TPU:0, one launch (start us, length us, event | category | flops | bytes accessed | tf_op | source)
XLA Modules:
  0.0 861.5 jit_solution(7300815515893598700)
XLA Ops:
  9.8 2.4 fusion.47
  14.1 4.8 copy.83
  18.9 2.7 reshape.379
  21.6 22.3 %all_to_all.63 = bf16[4,2,36864]{2,1,0:T(2,128)(2,1)} all-to-all(bf16[4,2,36864]{2,1,0:T(2,128)(2,1)} %reshape.379), channel_id=1, replica_groups=mesh['blk'=2,'head'=4,'weight'=4] {'head'}, dimensions={0} | all-to-all | bytes 1179648 | tf_op jit(solution)/shard_map/all_to_all | solution.py:92
  43.9 2.6 reshape.380
  46.6 4.8 copy.101
  54.5 2.0 fusion.66
  58.3 32.0 %all-gather.6.cloned.1.call-done = bf16[2048,2,2,192]{3,0,2,1:T(8,128)(2,1)} async-done(((bf16[256,2,2,192]{3,0,2,1:T(8,128)(2,1)}), bf16[2048,2,2,192]{3,0,2,1:T(8,128)(2,1)}) %all-gather.6.cloned.1.call-update) | async-done | bytes 3145744 | tf_op jit(solution)/shard_map/all_gather | solution.py:132
  90.3 6.1 copy.87
  96.4 23.2 %while.37 = (s32[]{:T(128)}, f32[256,2,3,64]{0,3,2,1:T(8,128)}, f32[2,3,256]{2,1,0:T(4,128)S(1)}, bf16[2048,2,2,192]{0,3,1,2:T(8,128)(2,1)}, s32[2]{0:T(128)}, /...) while((s32[]{:T(128)}, f32[256,2,3,64]{0,3,2,1:T(8,128)}, ...), condition=%wide.region_2.3_spmd.clone, body=%wide.region_0.2_spmd.clone.sunk | while | flops 412356096 | bytes 19118340 | solution.py:58
  96.4 2.4 constant_dynamic-slice_fusion.3
  99.6 3.5 bitcast_reduce_fusion.2
  103.1 4.8 fusion.121
  107.9 2.4 constant_dynamic-slice_fusion.3
  111.1 3.5 bitcast_reduce_fusion.2
  114.6 4.9 fusion.121
  123.1 13.9 %all_to_all.64 = bf16[256,2,192]{2,1,0:T(2,128)(2,1)S(1)} all-to-all(bf16[256,2,192]{2,1,0:T(2,128)(2,1)} %copy.88), channel_id=1, replica_groups=mesh['blk'=2,'head'=4,'weight'=4] {'head'}, dimensions={0} | all-to-all | bytes 393216 | tf_op jit(solution)/shard_map/all_to_all | solution.py:135
  145.3 9.5 %all_gather.28 = bf16[256,2,768]{2,1,0:T(2,128)(2,1)} all-gather(bf16[64,2,768]{2,1,0:T(2,128)(2,1)} %reshape.355), channel_id=1, replica_groups=mesh['blk'=2,'head'=4,'weight'=4] {'weight'}, dimensions={0}, use_global_device_ids=true | all-gather | bytes 983040 | tf_op jit(solution)/shard_map/all_gather | solution.py:150
  154.8 3.0 reshape.356
  157.8 3.6 multiply_convert_fusion.1
  164.0 2.9 convert_element_type.132
  174.7 26.6 %all-reduce.11.cloned.1.call-done = bf16[256,2,768]{2,1,0:T(2,128)(2,1)} async-done(((bf16[256,2,768]{2,1,0:T(2,128)(2,1)}), bf16[256,2,768]{2,1,0:T(2,128)(2,1)}) %all-reduce.11.cloned.1.call-update) | async-done | bytes 786448
  203.1 2.0 reshape.369
  212.2 9.3 %all_gather.31 = bf16[256,2,768]{2,1,0:T(2,128)(2,1)} all-gather(bf16[64,2,768]{2,1,0:T(2,128)(2,1)} %reshape.360), channel_id=1, replica_groups=mesh['blk'=2,'head'=4,'weight'=4] {'weight'}, dimensions={0}, use_global_device_ids=true | all-gather | bytes 983040 | tf_op jit(solution)/shard_map/all_gather | solution.py:180
  221.5 3.0 reshape.361
  224.4 3.8 fusion.69
  230.8 2.8 convert_element_type.142
  234.2 35.0 %all-reduce.13.cloned.1.call-done = bf16[256,2,768]{2,1,0:T(2,128)(2,1)} async-done(((bf16[256,2,768]{2,1,0:T(2,128)(2,1)}), bf16[256,2,768]{2,1,0:T(2,128)(2,1)}) %all-reduce.13.cloned.1.call-update) | async-done | bytes 786448
  271.1 2.0 reshape.372
  273.1 2.2 multiply_reduce_fusion.1
  280.4 2.0 copy.92
  284.4 11.5 %all_to_all.65 = bf16[4,2,12288]{2,1,0:T(2,128)(2,1)} all-to-all(bf16[4,2,12288]{2,1,0:T(2,128)(2,1)} %reshape.381), channel_id=1, replica_groups=mesh['blk'=2,'head'=4,'weight'=4] {'head'}, dimensions={0} | all-to-all | bytes 393216 | tf_op jit(solution)/shard_map/all_to_all | solution.py:217
  297.9 2.0 copy.105
  305.6 8.8 %all_gather.30 = bf16[2048,2,3]{0,2,1:T(4,128)(2,1)S(1)} all-gather(bf16[256,2,3]{0,2,1:T(4,128)(2,1)S(1)} %bitcast_convert_fusion.6), channel_id=1, replica_groups=mesh['blk'=2,'head'=4,'weight'=4] {'blk','weight'}, dimensions={0}, use_global_device_ids=true | all-gather | bytes 27648 | tf_op jit(solution)/shard_map/all_gather | solution.py:287
  316.2 8.6 %all_gather.33 = bf16[2048,2,3]{0,2,1:T(4,128)(2,1)S(1)} all-gather(bf16[256,2,3]{0,2,1:T(4,128)(2,1)S(1)} %multiply_reduce_fusion.2), channel_id=1, replica_groups=mesh['blk'=2,'head'=4,'weight'=4] {'blk','weight'}, dimensions={0}, use_global_device_ids=true | all-gather | bytes 27648 | tf_op jit(solution)/shard_map/all_gather | solution.py:284
  327.5 38.3 %while.38 = (s32[]{:T(128)}, f32[256,2,3,64]{0,3,2,1:T(8,128)}, f32[256,2,3,64]{0,3,2,1:T(8,128)}, bf16[2048,2,192]{0,2,1:T(8,128)(2,1)}, bf16[2048,2,3,64]{0,3,...) while((s32[]{:T(128)}, f32[256,2,3,64]{0,3,2,1:T(8,128)}, ...), condition=%wide.region_15.16_spmd.clone, body=%wide.region_14.15_spmd.clone.sunk | while | flops 1018921472 | bytes 103770656 | solution.py:58
  329.0 3.7 select_divide_fusion.2
  332.8 3.3 multiply_convert_fusion.3
  336.4 3.7 fusion.132
  340.1 3.7 fusion.133
  348.1 3.7 select_divide_fusion.2
  351.9 3.3 multiply_convert_fusion.3
  355.5 3.7 fusion.132
  359.3 3.7 fusion.133
  369.2 35.0 %reduce-scatter.2.cloned.1.call-done = bf16[256,2,192]{0,2,1:T(8,128)(2,1)} async-done(((bf16[2048,2,192]{0,2,1:T(8,128)(2,1)}), bf16[256,2,192]{0,2,1:T(8,128)(2,1)}) %reduce-scatter.2.cloned.1.call-update) | async-done | bytes 196624 | tf_op jit(solution)/shard_map/reduce_scatter | solution.py:292
  406.2 3.0 copy.96
  409.2 4.6 all-to-all-start.3
  413.8 3.2 convolution_convert_fusion
  417.1 3.0 fusion.57
  420.1 24.4 %all-to-all-done.3 = bf16[256,2,3,192]{3,1,2,0:T(2,128)(2,1)} async-done(((bf16[256,2,3,192]{3,1,2,0:T(2,128)(2,1)}), bf16[256,2,3,192]{3,1,2,0:T(2,128)(2,1)}, u32[]{:S(2)}, u32[]{:S(2)}) %all-to-all-start.3) | async-done | bytes 589856 | tf_op jit(solution)/shard_map/all_to_all | solution.py:298
  448.2 2.7 reshape.366
  450.8 5.2 convolution_bitcast_fusion
  456.1 3.2 convolution_convert_fusion.1
  461.0 19.4 %psum.91 = bf16[768]{0:T(1024)(128)(2,1)S(1)} all-reduce(bf16[768]{0:T(1024)(128)(2,1)S(1)} %copy-done.34), channel_id=1, replica_groups=mesh['blk'=2,'head'=4,'weight'=4] {'blk','head'}, use_global_device_ids=true, to_apply=%region_30.31 | all-reduce | flops 768 | bytes 3072 | tf_op jit(solution)/shard_map/psum | solution.py:323
  481.0 24.9 %all-reduce.9.cloned.1.call-done = bf16[768,768]{1,0:T(8,128)(2,1)} async-done(((bf16[768,768]{1,0:T(8,128)(2,1)}), bf16[768,768]{1,0:T(8,128)(2,1)}) %all-reduce.9.cloned.1.call-update) | async-done | bytes 1179664 | tf_op jit(solution)/shard_map/psum | solution.py:324
  505.9 2.9 convert_element_type.156
  508.8 2.0 convolution_add_fusion.3
  510.9 2.0 reshape.367
  517.5 42.9 %all-reduce.2 = (f32[768]{0:T(1024)}, f32[768]{0:T(1024)}, f32[768]{0:T(1024)}, f32[768]{0:T(1024)}, f32[768]{0:T(1024)}, /*index=5*/f32[768]{0:T(1024)}, f32[768]{0:T(1024)}, f32[768]{0:T(1024)}) all-reduce(f32[768]{0:T(1024)} %slice.53, f32[768]{0:T(1024)} %slice.55, ...), channel_id=1, replica_groups=mesh['blk'=2,'head'=4,'weight'=4] {'blk','head','weight'}, use_global_device_ids=true, to_apply=%region_19.20 | all-reduce | flops 6144 | bytes 49152 | tf_op jit(solution)/shard_map/psum | solution.py:306
  560.4 143.9 %all-reduce.15.cloned.1.call-done = (f32[768,2304]{0,1:T(8,128)}, f32[768,768]{1,0:T(8,128)}) async-done(((f32[768,2304]{0,1:T(8,128)}, f32[768,768]{1,0:T(8,128)}), (f32[768,2304]{0,1:T(8,128)}, f32[768,768]{1,0:T(8,128)})) %all-reduce.15.cloned.1.call-update) | async-done | bytes 9437200 | tf_op jit(solution)/shard_map/psum | solution.py:306
  704.3 8.0 copy.99
  712.3 132.0 %all-gather.12.cloned.1.call-done = bf16[6144,768]{1,0:T(8,128)(2,1)} async-done(((bf16[768,768]{1,0:T(8,128)(2,1)}), bf16[6144,768]{1,0:T(8,128)(2,1)}) %all-gather.12.cloned.1.call-update) | async-done | bytes 9437200 | tf_op jit(solution)/shard_map/all_gather | solution.py:14
  844.3 6.3 reduce_sum.195
  850.6 3.0 convert_element_type.152
  (205 shorter events, 92.1 us)
Async XLA Ops:
  7.2 2.6 copy-start
  7.2 83.1 %all-gather.6.cloned.1.call-start = ((), (), s32[]{:S(2)}) async-start(), calls=%async_computation.5 | async-start | bytes 4718592 | tf_op jit(solution)/shard_map/all_gather | solution.py:132
  52.7 0.9 copy-start.17
  54.4 146.8 %all-reduce.11.cloned.1.call-start = ((), (), s32[]{:S(2)}) async-start(), calls=%async_computation.11 | async-start | bytes 1572864
  96.4 3.2 copy-start.22
  99.5 3.5 copy-start.23
  107.9 3.2 copy-start.22
  111.1 3.5 copy-start.23
  137.0 5.8 copy-start.24
  137.0 5.8 copy-start.26
  141.6 0.8 copy-start.7
  141.6 0.7 copy-start.30
  142.3 0.5 copy-start.31
  143.6 14.1 %copy-start.37 = (f32[768]{0:T(1024)S(1)}, f32[768]{0:T(1024)}, u32[]{:S(2)}) copy-start(f32[768]{0:T(1024)} %param.29) | copy-start | bytes 9220
  157.8 4.6 copy-start.35
  161.4 1.0 copy-start.38
  164.0 4.9 copy-start.25
  166.9 102.3 %all-reduce.13.cloned.1.call-start = ((), (), s32[]{:S(2)}) async-start(), calls=%async_computation.12 | async-start | bytes 1572864
  205.1 1.7 copy-start.20
  205.1 2.4 copy-start.32
  205.1 2.4 copy-start.33
  209.0 0.7 copy-start.19
  224.4 4.6 copy-start.36
  228.2 0.9 copy-start.39
  233.6 91.8 %all-gather.8.cloned.1.call-start = ((), (), s32[]{:S(2)}) async-start(), calls=%async_computation.6 | async-start | bytes 1769472 | tf_op jit(solution)/shard_map/all_gather | solution.py:282
  234.2 92.0 %all-gather.10.cloned.1.call-start = ((), (), s32[]{:S(2)}) async-start(), calls=%async_computation.7 | async-start | bytes 1769472 | tf_op jit(solution)/shard_map/all_gather | solution.py:283
  273.1 2.2 copy-start.8
  273.1 4.4 copy-start.18
  276.7 0.7 copy-start.15
  301.9 102.3 %reduce-scatter.2.cloned.1.call-start = ((), (), s32[]{:S(2)}) async-start(), calls=%async_computation.8 | async-start | bytes 1769472 | tf_op jit(solution)/shard_map/reduce_scatter | solution.py:292
  329.0 3.8 copy-start.3
  329.0 3.8 copy-start.12
  332.8 3.7 copy-start.2
  336.4 3.7 copy-start.4
  336.4 3.7 copy-start.5
  340.1 3.8 copy-start.1
  340.1 3.8 copy-start.10
  343.8 1.1 copy-start.6
  343.9 1.5 copy-start.13
  345.5 1.1 copy-start.14
  348.1 3.8 copy-start.3
  348.1 3.8 copy-start.12
  351.9 3.7 copy-start.2
  355.5 3.7 copy-start.4
  355.5 3.7 copy-start.5
  359.3 3.8 copy-start.1
  359.3 3.8 copy-start.10
  363.0 1.1 copy-start.6
  363.0 1.5 copy-start.13
  364.6 1.1 copy-start.14
  409.2 35.3 %all-to-all-start.3 = ((bf16[256,2,3,192]{3,1,2,0:T(2,128)(2,1)}), bf16[256,2,3,192]{3,1,2,0:T(2,128)(2,1)}, u32[]{:S(2)}, u32[]{:S(2)}) async-start(bf16[256,2,3,192]{3,1,2,0:T(2,128)(2,1)} %copy.96), calls=%async_computation.4 | async-start | bytes 1572864 | tf_op jit(solution)/shard_map/all_to_all | solution.py:298
  413.8 92.1 %all-reduce.9.cloned.1.call-start = ((), (), s32[]{:S(2)}) async-start(), calls=%async_computation.9 | async-start | bytes 2359296 | tf_op jit(solution)/shard_map/psum | solution.py:324
  417.0 287.3 %all-reduce.15.cloned.1.call-start = ((), (), s32[]{:S(2)}) async-start(), calls=%async_computation.13 | async-start | bytes 18874368 | tf_op jit(solution)/shard_map/psum | solution.py:306
  445.8 0.9 copy-start.11
  456.0 388.3 %all-gather.12.cloned.1.call-start = ((), (), s32[]{:S(2)}) async-start(), calls=%async_computation.10 | async-start | bytes 10616832 | tf_op jit(solution)/shard_map/all_gather | solution.py:14
  459.3 1.7 copy-start.34
  505.9 2.9 copy-start.9
  505.9 2.9 copy-start.16
  510.9 6.6 copy-start.27
  510.9 6.6 copy-start.28
  510.9 6.6 copy-start.29
  850.6 3.0 copy-start.21
Sparse Core Ops, SparseCore 0:
  54.6 35.6 all-gather.5
  167.0 34.2 all-reduce.10
  233.7 35.4 all-reduce.12
  271.0 25.7 all-gather.7
  302.0 24.0 all-gather.9
  365.9 38.2 reduce-scatter.1
  418.7 87.1 all-reduce.8
  513.0 191.2 all-reduce.14
  707.0 137.2 all-gather.11
